TPU v7x, 32 devices: a whole 2x2x4 slice. The times are simulated.
32 devices in a mesh: dp: 8 (over z, core), tensor: 4 (over y, x).
Axes of the slice: x: 2, y: 2, z: 4, core: 2. Of those that a mesh axis runs over, the one named last changes fastest.
Arguments:
- tokens: bfloat16 [8192, 2048], P('dp'), may hold values from -6 to 6
- cotangent: bfloat16 [8192, 2048], P('dp'), may hold values from -6 to 6
- seq_lengths: int32 [4], replicated, may hold values from 1536 to 2048, as said below
- slot_seq: int32 [4], replicated, may hold values from 0 to 3, each once
- w_query: float32 [2048, 2048], P('dp', 'tensor'), may hold values from -0.125 to 0.125
- w_key: float32 [2048, 2048], P('dp', 'tensor'), may hold values from -0.125 to 0.125
- w_value: float32 [2048, 2048], P('dp', 'tensor'), may hold values from -0.125 to 0.125
- b_query: float32 [2048], P('tensor'), may hold values from -3 to 3
- b_value: float32 [2048], P('tensor'), may hold values from -3 to 3
- w_out: float32 [2048, 2048], P('tensor', 'dp'), may hold values from -4 to 4
- b_out: float32 [2048], replicated, may hold values from -3 to 3
- ln1_gain: float32 [2048], replicated, may hold values from 0.5 to 1.5
- ln1_bias: float32 [2048], replicated, may hold values from -3 to 3
- w_inner: float32 [2048, 8192], P('dp', 'tensor'), may hold values from -0.125 to 0.125
- b_inner: float32 [8192], P('tensor'), may hold values from -3 to 3
- w_outer: float32 [8192, 2048], P('tensor', 'dp'), may hold values from -0.0625 to 0.0625
- b_outer: float32 [2048], replicated, may hold values from -3 to 3
- ln2_gain: float32 [2048], replicated, may hold values from 0.5 to 1.5
- ln2_bias: float32 [2048], replicated, may hold values from -3 to 3
Outputs:
- output: float32 [8192, 2048], P('dp')
- grad_tokens: float32 [8192, 2048], P('dp')
- grad_w_query: float32 [2048, 2048], P('dp', 'tensor')
- grad_w_key: float32 [2048, 2048], P('dp', 'tensor')
- grad_w_value: float32 [2048, 2048], P('dp', 'tensor')
- grad_b_query: float32 [2048], P('tensor')
- grad_b_value: float32 [2048], P('tensor')
- grad_w_out: float32 [2048, 2048], P('tensor', 'dp')
- grad_b_out: float32 [2048], replicated
- grad_ln1_gain: float32 [2048], replicated
- grad_ln1_bias: float32 [2048], replicated
- grad_w_inner: float32 [2048, 8192], P('dp', 'tensor')
- grad_b_inner: float32 [8192], P('tensor')
- grad_w_outer: float32 [8192, 2048], P('tensor', 'dp')
- grad_b_outer: float32 [2048], replicated
- grad_ln2_gain: float32 [2048], replicated
- grad_ln2_bias: float32 [2048], replicated
Inputs may be any that keep to these rules, and one draw needn't show every extreme that they name: `seq_lengths`: each sequence's valid tokens; some sequence has exactly 2048 and some exactly 1536. `slot_seq`: each sequence stands in exactly one slot.
All inputs are finite; a program needn't handle non-finite values.
Results may differ from a plain program's by a relative error of at most 0.019.
Values may be sent and summed in bfloat16 or wider, within the bound.
No kernel may reach another device: no remote copies, remote signals or barrier semaphores. Data moves between devices by JAX's collectives and lax.ppermute only.
A program may use at most 256 MiB of HBM per device.

v0:
```python
import jax
import jax.numpy as jnp
from jax import lax
from jax.sharding import PartitionSpec as P

HEAD_DIM = 128
SLOT = 2048
norm_eps = 1e-12


def passed_along(value, axis, steps):
    count = lax.axis_size(axis)
    leading, last = (max(0, -steps), min(count, count - steps))
    return lax.ppermute(value, axis, [(source, source + steps) for source in range(leading, last)])


def layer_norm(resid, gain, shift):
    center = resid - jnp.mean(resid, axis=-1, keepdims=True)
    spread = jnp.mean(center * center, axis=-1, keepdims=True)
    return center * lax.rsqrt(spread + norm_eps) * gain + shift


def gelu_tanh(inner):
    return 0.5 * inner * (1.0 + jnp.tanh(0.7978845608 * (inner + 0.044715 * inner * inner * inner)))


def mat_bf(left, right):
    return jnp.dot(left, right, preferred_element_type=jnp.float32)


def tensor_total(part):
    return lax.psum(part, "tensor")


def on_device(
    tokens,
    cotangent,
    seq_lengths,
    slot_seq,
    w_query,
    w_key,
    w_value,
    b_query,
    b_value,
    w_out,
    b_out,
    ln1_gain,
    ln1_bias,
    w_inner,
    b_inner,
    w_outer,
    b_outer,
    ln2_gain,
    ln2_bias,
):
    tok_rows = tokens.shape[0]
    shard_count = SLOT // tok_rows
    width_here = w_query.shape[1]
    heads_here = width_here // HEAD_DIM
    score_scale = HEAD_DIM ** (-0.5)
    block_rows = min(512, tok_rows)
    block_count = tok_rows // block_rows
    dp_place = lax.axis_index("dp")
    my_slot = dp_place // shard_count
    my_spot = dp_place % shard_count
    slot_ids = jnp.arange(slot_seq.shape[0])
    slot_lengths = jnp.sum(
        jnp.where(slot_seq[:, None] == slot_ids[None, :], seq_lengths[None, :], 0), axis=1
    )
    my_length = jnp.sum(jnp.where(slot_ids == my_slot, slot_lengths, 0))
    row_live = (my_spot * tok_rows + jnp.arange(tok_rows) < my_length).astype(jnp.float32)
    key_live = jnp.arange(SLOT) < my_length
    spot_ids = jnp.arange(shard_count)
    offset_list = [step_by for step_by in range(1 - shard_count, shard_count) if step_by != 0]
    own_hit = (spot_ids == my_spot)[:, None, None]
    tokens_wide = tokens.astype(jnp.float32)
    cot_wide = cotangent.astype(jnp.float32)
    full_query, full_key, full_value, full_out = (
        lax.all_gather(w_query.astype(jnp.bfloat16), "dp", axis=0, tiled=True),
        lax.all_gather(w_key.astype(jnp.bfloat16), "dp", axis=0, tiled=True),
        lax.all_gather(w_value.astype(jnp.bfloat16), "dp", axis=0, tiled=True),
        lax.all_gather(w_out.astype(jnp.bfloat16), "dp", axis=1, tiled=True),
    )
    query_rows = (mat_bf(tokens, full_query) + b_query).astype(jnp.bfloat16)
    key_rows = mat_bf(tokens, full_key).astype(jnp.bfloat16)
    value_rows = (mat_bf(tokens, full_value) + b_value).astype(jnp.bfloat16)
    empty_slab = jnp.zeros((shard_count, tok_rows, width_here), jnp.bfloat16)
    key_slab = jnp.where(own_hit, key_rows[None], empty_slab)
    value_slab = jnp.where(own_hit, value_rows[None], empty_slab)
    for step_by in offset_list:
        far_key, far_value = passed_along((key_rows, value_rows), "dp", step_by)
        far_hit = (spot_ids == my_spot - step_by)[:, None, None]
        key_slab = jnp.where(far_hit, far_key[None], key_slab)
        value_slab = jnp.where(far_hit, far_value[None], value_slab)
    slot_keys = key_slab.reshape(SLOT, heads_here, HEAD_DIM)
    slot_values = value_slab.reshape(SLOT, heads_here, HEAD_DIM)
    query_blocks = query_rows.reshape(block_count, block_rows, heads_here, HEAD_DIM)

    def score_block(query_part):
        scores = (
            jnp.einsum("qhd,khd->hqk", query_part, slot_keys, preferred_element_type=jnp.float32)
            * score_scale
        )
        return jnp.where(key_live[None, None, :], scores, -1e30)

    def forward_block(query_part):
        scores = score_block(query_part)
        top = jnp.max(scores, axis=-1, keepdims=True)
        expd = jnp.exp(scores - top)
        total = jnp.sum(expd, axis=-1, keepdims=True)
        probs = expd / total
        mixed = jnp.einsum(
            "hqk,khd->qhd",
            probs.astype(jnp.bfloat16),
            slot_values,
            preferred_element_type=jnp.float32,
        )
        return (mixed, top + jnp.log(total))

    mixed_blocks, lse_blocks = lax.map(forward_block, query_blocks)
    heads_rows = mixed_blocks.reshape(tok_rows, width_here).astype(jnp.bfloat16)
    attn_part = mat_bf(heads_rows, full_out)
    attn = tensor_total(attn_part) + b_out
    resid_one = tokens_wide + attn
    hidden, norm_one_back = jax.vjp(layer_norm, resid_one, ln1_gain, ln1_bias)
    hidden_low = hidden.astype(jnp.bfloat16)
    full_inner, full_outer = (
        lax.all_gather(w_inner.astype(jnp.bfloat16), "dp", axis=0, tiled=True),
        lax.all_gather(w_outer.astype(jnp.bfloat16), "dp", axis=1, tiled=True),
    )
    inner = mat_bf(hidden_low, full_inner) + b_inner
    act_low = gelu_tanh(inner).astype(jnp.bfloat16)
    outer_part = mat_bf(act_low, full_outer)
    outer = tensor_total(outer_part) + b_outer
    output, norm_two_back = jax.vjp(layer_norm, hidden + outer, ln2_gain, ln2_bias)
    grad_out = cot_wide * row_live[:, None]
    grad_two, grad_ln2_gain, grad_ln2_bias = norm_two_back(grad_out)
    back_inner, back_outer = (
        lax.all_gather(w_inner.astype(jnp.bfloat16), "dp", axis=0, tiled=True),
        lax.all_gather(w_outer.astype(jnp.bfloat16), "dp", axis=1, tiled=True),
    )
    outer_low = grad_two.astype(jnp.bfloat16)
    grad_b_outer = jnp.sum(grad_two, axis=0)
    grad_w_outer = jnp.einsum("tf,td->fd", act_low, outer_low, preferred_element_type=jnp.float32)
    grad_act = jnp.einsum("td,fd->tf", outer_low, back_outer, preferred_element_type=jnp.float32)
    gelu_value, gelu_back = jax.vjp(gelu_tanh, inner)
    inner_low = gelu_back(grad_act)[0].astype(jnp.bfloat16)
    grad_b_inner = jnp.sum(inner_low.astype(jnp.float32), axis=0)
    grad_w_inner = jnp.einsum(
        "td,tf->df", hidden_low, inner_low, preferred_element_type=jnp.float32
    )
    grad_w_inner, grad_w_outer = (
        lax.psum_scatter(
            grad_w_inner.astype(jnp.bfloat16), "dp", scatter_dimension=0, tiled=True
        ).astype(jnp.float32),
        lax.psum_scatter(
            grad_w_outer.astype(jnp.bfloat16), "dp", scatter_dimension=1, tiled=True
        ).astype(jnp.float32),
    )
    hidden_part = jnp.einsum("tf,df->td", inner_low, back_inner, preferred_element_type=jnp.float32)
    grad_hidden = grad_two + tensor_total(hidden_part)
    grad_one, grad_ln1_gain, grad_ln1_bias = norm_one_back(grad_hidden)
    attn_low = grad_one.astype(jnp.bfloat16)
    grad_b_out = jnp.sum(grad_one, axis=0)
    back_query, back_key, back_value, back_out = (
        lax.all_gather(w_query.astype(jnp.bfloat16), "dp", axis=0, tiled=True),
        lax.all_gather(w_key.astype(jnp.bfloat16), "dp", axis=0, tiled=True),
        lax.all_gather(w_value.astype(jnp.bfloat16), "dp", axis=0, tiled=True),
        lax.all_gather(w_out.astype(jnp.bfloat16), "dp", axis=1, tiled=True),
    )
    grad_w_out = jnp.einsum("tc,td->cd", heads_rows, attn_low, preferred_element_type=jnp.float32)
    mixed_low = jnp.einsum(
        "td,cd->tc", attn_low, back_out, preferred_element_type=jnp.float32
    ).astype(jnp.bfloat16)
    grad_blocks = mixed_low.reshape(block_count, block_rows, heads_here, HEAD_DIM)

    def backward_block(carry, inputs):
        key_sum, value_sum = carry
        query_part, grad_part, lse_part = inputs
        probs = jnp.exp(score_block(query_part) - lse_part)
        grad_probs = jnp.einsum(
            "qhd,khd->hqk", grad_part, slot_values, preferred_element_type=jnp.float32
        )
        inner_sum = jnp.sum(probs * grad_probs, axis=-1, keepdims=True)
        score_low = (probs * (grad_probs - inner_sum)).astype(jnp.bfloat16)
        grad_query = (
            jnp.einsum("hqk,khd->qhd", score_low, slot_keys, preferred_element_type=jnp.float32)
            * score_scale
        )
        key_sum = (
            key_sum
            + jnp.einsum("hqk,qhd->khd", score_low, query_part, preferred_element_type=jnp.float32)
            * score_scale
        )
        value_sum = value_sum + jnp.einsum(
            "hqk,qhd->khd",
            probs.astype(jnp.bfloat16),
            grad_part,
            preferred_element_type=jnp.float32,
        )
        return ((key_sum, value_sum), grad_query)

    zero_slab = jnp.zeros((SLOT, heads_here, HEAD_DIM), jnp.float32)
    (key_sum, value_sum), grad_query_blocks = lax.scan(
        backward_block, (zero_slab, zero_slab), (query_blocks, grad_blocks, lse_blocks)
    )
    key_grad_slab = key_sum.reshape(shard_count, tok_rows, width_here)
    value_grad_slab = value_sum.reshape(shard_count, tok_rows, width_here)
    grad_key = jnp.sum(jnp.where(own_hit, key_grad_slab, 0.0), axis=0)
    grad_value = jnp.sum(jnp.where(own_hit, value_grad_slab, 0.0), axis=0)
    for step_by in offset_list:
        far_hit = (spot_ids == my_spot - step_by)[:, None, None]
        send_key = jnp.sum(jnp.where(far_hit, key_grad_slab, 0.0), axis=0)
        send_value = jnp.sum(jnp.where(far_hit, value_grad_slab, 0.0), axis=0)
        back_key_rows, back_value_rows = (
            passed_along(send_key.astype(jnp.bfloat16), "dp", -step_by).astype(send_key.dtype),
            passed_along(send_value.astype(jnp.bfloat16), "dp", -step_by).astype(send_value.dtype),
        )
        grad_key = grad_key + back_key_rows
        grad_value = grad_value + back_value_rows
    query_low = grad_query_blocks.reshape(tok_rows, width_here).astype(jnp.bfloat16)
    key_low = grad_key.astype(jnp.bfloat16)
    value_low = grad_value.astype(jnp.bfloat16)
    grad_w_query = jnp.einsum("td,tc->dc", tokens, query_low, preferred_element_type=jnp.float32)
    grad_w_key = jnp.einsum("td,tc->dc", tokens, key_low, preferred_element_type=jnp.float32)
    grad_w_value = jnp.einsum("td,tc->dc", tokens, value_low, preferred_element_type=jnp.float32)
    grad_b_query = jnp.sum(query_low.astype(jnp.float32), axis=0)
    grad_b_value = jnp.sum(value_low.astype(jnp.float32), axis=0)
    input_part = jnp.einsum("tc,dc->td", query_low, back_query, preferred_element_type=jnp.float32)
    input_part = input_part + jnp.einsum(
        "tc,dc->td", key_low, back_key, preferred_element_type=jnp.float32
    )
    input_part = input_part + jnp.einsum(
        "tc,dc->td", value_low, back_value, preferred_element_type=jnp.float32
    )
    grad_tokens = grad_one + tensor_total(input_part)
    grad_w_query, grad_w_key, grad_w_value, grad_w_out = (
        lax.psum_scatter(
            grad_w_query.astype(jnp.bfloat16), "dp", scatter_dimension=0, tiled=True
        ).astype(jnp.float32),
        lax.psum_scatter(
            grad_w_key.astype(jnp.bfloat16), "dp", scatter_dimension=0, tiled=True
        ).astype(jnp.float32),
        lax.psum_scatter(
            grad_w_value.astype(jnp.bfloat16), "dp", scatter_dimension=0, tiled=True
        ).astype(jnp.float32),
        lax.psum_scatter(
            grad_w_out.astype(jnp.bfloat16), "dp", scatter_dimension=1, tiled=True
        ).astype(jnp.float32),
    )
    (
        grad_b_query,
        grad_b_value,
        grad_b_inner,
        grad_b_out,
        grad_b_outer,
        grad_ln1_gain,
        grad_ln1_bias,
        grad_ln2_gain,
        grad_ln2_bias,
    ) = (
        lax.psum(grad_b_query.astype(jnp.bfloat16), "dp").astype(jnp.float32),
        lax.psum(grad_b_value.astype(jnp.bfloat16), "dp").astype(jnp.float32),
        lax.psum(grad_b_inner.astype(jnp.bfloat16), "dp").astype(jnp.float32),
        lax.psum(grad_b_out.astype(jnp.bfloat16), "dp").astype(jnp.float32),
        lax.psum(grad_b_outer.astype(jnp.bfloat16), "dp").astype(jnp.float32),
        lax.psum(grad_ln1_gain.astype(jnp.bfloat16), "dp").astype(jnp.float32),
        lax.psum(grad_ln1_bias.astype(jnp.bfloat16), "dp").astype(jnp.float32),
        lax.psum(grad_ln2_gain.astype(jnp.bfloat16), "dp").astype(jnp.float32),
        lax.psum(grad_ln2_bias.astype(jnp.bfloat16), "dp").astype(jnp.float32),
    )
    return (
        output,
        grad_tokens,
        grad_w_query,
        grad_w_key,
        grad_w_value,
        grad_b_query,
        grad_b_value,
        grad_w_out,
        grad_b_out,
        grad_ln1_gain,
        grad_ln1_bias,
        grad_w_inner,
        grad_b_inner,
        grad_w_outer,
        grad_b_outer,
        grad_ln2_gain,
        grad_ln2_bias,
    )


def solution(mesh):
    return jax.shard_map(
        on_device,
        mesh=mesh,
        in_specs=(
            P("dp", None),
            P("dp", None),
            P(),
            P(),
            P("dp", "tensor"),
            P("dp", "tensor"),
            P("dp", "tensor"),
            P("tensor"),
            P("tensor"),
            P("tensor", "dp"),
            P(),
            P(),
            P(),
            P("dp", "tensor"),
            P("tensor"),
            P("tensor", "dp"),
            P(),
            P(),
            P(),
        ),
        out_specs=(
            P("dp", None),
            P("dp", None),
            P("dp", "tensor"),
            P("dp", "tensor"),
            P("dp", "tensor"),
            P("tensor"),
            P("tensor"),
            P("tensor", "dp"),
            P(),
            P(),
            P(),
            P("dp", "tensor"),
            P("tensor"),
            P("tensor", "dp"),
            P(),
            P(),
            P(),
        ),
        check_vma=False,
    )
```

profile of v0, /device:TPU:0, one launch (start us, length us, event | category | flops | bytes accessed | tf_op | source)
XLA Modules:
  0.0 1807.7 jit_solution(10736105335624038911)
XLA Ops:
  14.7 27.4 %all-gather.9.cloned.1.call-done = bf16[2048,512]{1,0:T(8,128)(2,1)} async-done(((bf16[256,512]{1,0:T(8,128)(2,1)}), bf16[2048,512]{1,0:T(8,128)(2,1)}) %all-gather.9.cloned.1.call-update) | async-done | bytes 2097168 | tf_op jit(solution)/shard_map/all_gather | solution.py:80
  52.8 25.2 %all-gather.11.cloned.1.call-done = bf16[2048,512]{1,0:T(8,128)(2,1)} async-done(((bf16[256,512]{1,0:T(8,128)(2,1)}), bf16[2048,512]{1,0:T(8,128)(2,1)}) %all-gather.11.cloned.1.call-update) | async-done | bytes 2097168 | tf_op jit(solution)/shard_map/all_gather | solution.py:81
  90.7 26.6 %all-gather.7.cloned.1.call-done = bf16[2048,512]{1,0:T(8,128)(2,1)} async-done(((bf16[256,512]{1,0:T(8,128)(2,1)}), bf16[2048,512]{1,0:T(8,128)(2,1)}) %all-gather.7.cloned.1.call-update) | async-done | bytes 2097168 | tf_op jit(solution)/shard_map/all_gather | solution.py:79
  127.6 128.1 %while.31 = (s32[]{:T(128)}, bf16[2,512,4,128]{3,1,2,0:T(8,128)(2,1)}, f32[2,4,512,1]{2,1,3,0:T(4,128)S(1)}, bf16[2,512,4,128]{3,1,2,0:T(8,128)(2,1)}, s32[]{:T(...) while((s32[]{:T(128)}, ...), condition=%wide.region_5.6_spmd.clone.clone, body=%wide.region_2.5_spmd.clone.clone.sunk | while | flops 2204106752 | bytes 137967920 | solution.py:120
  164.7 14.5 select_select_fusion.6
  228.7 14.5 select_select_fusion.6
  271.7 169.3 %all-reduce.6.cloned.1.call-done = f32[1024,2048]{1,0:T(8,128)} async-done(((f32[1024,2048]{1,0:T(8,128)}), f32[1024,2048]{1,0:T(8,128)}) %all-reduce.6.cloned.1.call-update) | async-done | bytes 8388624 | tf_op jit(solution)/shard_map/psum | solution.py:32
  451.1 74.8 %all-gather.15.cloned.1.call-done = bf16[2048,2048]{1,0:T(8,128)(2,1)} async-done(((bf16[256,2048]{1,0:T(8,128)(2,1)}), bf16[2048,2048]{1,0:T(8,128)(2,1)}) %all-gather.15.cloned.1.call-update) | async-done | bytes 8388624 | tf_op jit(solution)/shard_map/all_gather | solution.py:128
  525.9 15.8 fusion.87
  541.7 67.5 %all-gather.17.cloned.1.call-done = bf16[2048,2048]{1,0:T(8,128)(2,1)} async-done(((bf16[2048,256]{1,0:T(8,128)(2,1)}), bf16[2048,2048]{1,0:T(8,128)(2,1)}) %all-gather.17.cloned.1.call-update) | async-done | bytes 8388624 | tf_op jit(solution)/shard_map/all_gather | solution.py:129
  609.2 17.3 fusion.85
  627.5 169.5 %all-reduce.8.cloned.1.call-done = f32[1024,2048]{1,0:T(8,128)} async-done(((f32[1024,2048]{1,0:T(8,128)}), f32[1024,2048]{1,0:T(8,128)}) %all-reduce.8.cloned.1.call-update) | async-done | bytes 8388624 | tf_op jit(solution)/shard_map/psum | solution.py:32
  818.5 23.4 %fusion.94 = (bf16[2048]{0:T(1024)(128)(2,1)}, bf16[1024,2048]{1,0:T(8,128)(2,1)}) fusion(bf16[2048,2048]{1,0:T(8,128)(2,1)} %all-gather.17.cloned.1.call-done, f32[1024,2048]{1,0:T(8,128)} %get-tuple-element.655, f32[1024]{0:T(1024)S(1)} %negate_multiply_fusion.1, f32[1024,2048]{1,0:T(8,128)} %fusion.87, f32[2048]{0:T(1024)S(1)} %copy-done.68), kind=kOutput, calls=%fused_computation.149 | convolution fusion | flops 8648652800 | bytes 29376512 | tf_op jit(solution)/shard_map/td,fd->tf/dot_general | solution.py:145
  842.0 14.5 fusion.95
  856.5 172.9 %all-reduce.10.cloned.1.call-done = f32[1024,2048]{1,0:T(8,128)} async-done(((f32[1024,2048]{1,0:T(8,128)}), f32[1024,2048]{1,0:T(8,128)}) %all-reduce.10.cloned.1.call-update) | async-done | bytes 8388624 | tf_op jit(solution)/shard_map/psum | solution.py:32
  1029.4 11.8 multiply_reduce_fusion.2
  1061.4 165.6 %while.32 = (s32[]{:T(128)}, f32[2048,4,128]{0,2,1:T(8,128)}, f32[2048,4,128]{0,2,1:T(8,128)}, bf16[2,512,4,128]{3,1,2,0:T(8,128)(2,1)}, bf16[2,512,4,128]{3,1,2...) while((s32[]{:T(128)}, f32[2048,4,128]{0,2,1:T(8,128)}, ...), condition=%wide.region_19.20_spmd.clone.clone.clone, body=%wide.region_17.19_spmd.clone.clone.clone.sunk | while | flops 5443420160 | bytes 367073888 | solution.py:204
  1082.1 14.4 select_select_fusion.7
  1111.6 11.6 multiply_reduce_fusion.8
  1123.2 12.9 multiply_convert_fusion.5
  1163.9 14.4 select_select_fusion.7
  1194.9 11.6 multiply_reduce_fusion.8
  1206.5 12.9 multiply_convert_fusion.5
  1249.2 47.1 %select_reduce_fusion.4 = (bf16[1024,512]{0,1:T(8,128)(2,1)}, bf16[1024,512]{0,1:T(8,128)(2,1)}, f32[1024,512]{0,1:T(8,128)S(1)}, f32[1024,512]{0,1:T(8,128)S(1)...) fusion(f32[2,1024,512]{1,0,2:T(2,128)} %reshape.188, pred[2]{0:T(512)(128)(4,1)S(1)} %copy-done.63, ...), kind=kLoop, calls=%fused_computation.97 | loop fusion | flops 9437184 | bytes 16777222 | tf_op jit(solution)/shard_map/reduce_sum | solution.py:213
  1307.3 12.6 collective-permute-start.4
  1334.2 15.4 convolution_convert_fusion.1
  1350.3 20.0 %convolution_convert_fusion = bf16[2048,2048]{1,0:T(8,128)(2,1)} fusion(f32[1024,2048]{1,0:T(8,128)} %get-tuple-element.655, f32[1024]{0:T(1024)S(1)} %copy-done.54, f32[1024,2048]{1,0:T(8,128)} %fusion.87, f32[2048]{0:T(1024)S(1)} %copy-done.69), kind=kOutput, calls=%fused_computation.84 | convolution fusion | flops 8619294720 | bytes 25178112 | tf_op jit(solution)/shard_map/tf,td->fd/dot_general | solution.py:144
  1391.1 10.2 reduce-scatter.9.cloned.1.call-done
  1403.1 88.7 %reduce-scatter.15.cloned.1.call-done = bf16[256,2048]{1,0:T(8,128)(2,1)} async-done(((bf16[2048,2048]{1,0:T(8,128)(2,1)}), bf16[256,2048]{1,0:T(8,128)(2,1)}) %reduce-scatter.15.cloned.1.call-update) | async-done | bytes 1048592 | tf_op jit(solution)/shard_map/reduce_scatter | solution.py:153
  1494.7 87.5 %reduce-scatter.17.cloned.1.call-done = bf16[2048,256]{1,0:T(8,128)(2,1)} async-done(((bf16[2048,2048]{1,0:T(8,128)(2,1)}), bf16[2048,256]{1,0:T(8,128)(2,1)}) %reduce-scatter.17.cloned.1.call-update) | async-done | bytes 1048592 | tf_op jit(solution)/shard_map/reduce_scatter | solution.py:156
  1584.9 172.1 %all-reduce.12.cloned.1.call-done = f32[1024,2048]{1,0:T(8,128)} async-done(((f32[1024,2048]{1,0:T(8,128)}), f32[1024,2048]{1,0:T(8,128)}) %all-reduce.12.cloned.1.call-update) | async-done | bytes 8388624 | tf_op jit(solution)/shard_map/psum | solution.py:32
  1767.0 28.6 %all-reduce = (bf16[512]{0:T(512)(128)(2,1)S(1)}, bf16[512]{0:T(512)(128)(2,1)S(1)}, bf16[2048]{0:T(1024)(128)(2,1)S(1)}, bf16[2048]{0:T(1024)(128)(2,1)S(1)}, b...) all-reduce(bf16[512]{0:T(512)(128)(2,1)S(1)} %bitcast.117, ...), channel_id=1, replica_groups=mesh['dp'=8,'tensor'=4] {'dp'}, use_global_device_ids=true, to_apply=%region_31.32 | all-reduce | flops 15360 | bytes 61440 | tf_op jit(solution)/shard_map/psum | solution.py:262
  (384 shorter events, 386.8 us)
Async XLA Ops:
  7.2 34.8 %all-gather.9.cloned.1.call-start = ((), (), s32[]{:S(2)}) async-start(), calls=%async_computation.7 | async-start | bytes 2359296 | tf_op jit(solution)/shard_map/all_gather | solution.py:80
  9.0 68.9 %all-gather.11.cloned.1.call-start = ((), (), s32[]{:S(2)}) async-start(), calls=%async_computation.8 | async-start | bytes 2359296 | tf_op jit(solution)/shard_map/all_gather | solution.py:81
  10.9 106.4 %all-gather.7.cloned.1.call-start = ((), (), s32[]{:S(2)}) async-start(), calls=%async_computation.6 | async-start | bytes 2359296 | tf_op jit(solution)/shard_map/all_gather | solution.py:79
  12.7 245.8 %all-gather.13.cloned.1.call-start = ((), (), s32[]{:S(2)}) async-start(), calls=%async_computation.9 | async-start | bytes 2359296 | tf_op jit(solution)/shard_map/all_gather | solution.py:82
  14.6 426.4 %all-reduce.6.cloned.1.call-start = ((), (), s32[]{:S(2)}) async-start(), calls=%async_computation.10 | async-start | bytes 16777216 | tf_op jit(solution)/shard_map/psum | solution.py:32
  47.3 79.2 %collective-permute-start.1 = (bf16[1024,512]{1,0:T(8,128)(2,1)S(1)}, bf16[1024,512]{1,0:T(8,128)(2,1)}, u32[]{:S(2)}, u32[]{:S(2)}) collective-permute-start(bf16[1024,512]{1,0:T(8,128)(2,1)S(1)} %convolution_convert_fusion.7), channel_id=1, source_target_pairs={{4,0},{8,4},{12,8},{16,12},{20,16},{24,20},{28,24},{5,1},{9,5},{13... | collective-permute-start | bytes 3145736 | tf_op jit(solution)/shard_map/ppermute | solution.py:14
  48.7 77.7 %collective-permute-start = (bf16[1024,512]{1,0:T(8,128)(2,1)S(1)}, bf16[1024,512]{1,0:T(8,128)(2,1)}, u32[]{:S(2)}, u32[]{:S(2)}) collective-permute-start(bf16[1024,512]{1,0:T(8,128)(2,1)S(1)} %convolution_convert_fusion.7), channel_id=1, source_target_pairs={{0,4},{4,8},{8,12},{12,16},{16,20},{20,24},{24,28},{1,5},{5,9},{9,... | collective-permute-start | bytes 3145736 | tf_op jit(solution)/shard_map/ppermute | solution.py:14
  83.2 43.3 %collective-permute-start.3 = (bf16[1024,512]{1,0:T(8,128)(2,1)S(1)}, bf16[1024,512]{1,0:T(8,128)(2,1)}, u32[]{:S(2)}, u32[]{:S(2)}) collective-permute-start(bf16[1024,512]{1,0:T(8,128)(2,1)S(1)} %add_convert_fusion.4), channel_id=1, source_target_pairs={{4,0},{8,4},{12,8},{16,12},{20,16},{24,20},{28,24},{5,1},{9,5},{13... | collective-permute-start | bytes 3145736 | tf_op jit(solution)/shard_map/ppermute | solution.py:14
  84.5 42.0 %collective-permute-start.2 = (bf16[1024,512]{1,0:T(8,128)(2,1)S(1)}, bf16[1024,512]{1,0:T(8,128)(2,1)}, u32[]{:S(2)}, u32[]{:S(2)}) collective-permute-start(bf16[1024,512]{1,0:T(8,128)(2,1)S(1)} %add_convert_fusion.4), channel_id=1, source_target_pairs={{0,4},{4,8},{8,12},{12,16},{16,20},{20,24},{24,28},{1,5},{5,9},{9,... | collective-permute-start | bytes 3145736 | tf_op jit(solution)/shard_map/ppermute | solution.py:14
  255.7 191.0 %copy-start.12 = (bf16[1024,512]{1,0:T(8,128)(2,1)}, bf16[1024,512]{1,0:T(8,128)(2,1)S(1)}, u32[]{:S(2)}) copy-start(bf16[1024,512]{1,0:T(8,128)(2,1)S(1)} %get-tuple-element.1027) | copy-start | bytes 3145732
  265.9 260.0 %all-gather.15.cloned.1.call-start = ((), (), s32[]{:S(2)}) async-start(), calls=%async_computation.11 | async-start | bytes 9437184 | tf_op jit(solution)/shard_map/all_gather | solution.py:128
  268.7 340.5 %all-gather.17.cloned.1.call-start = ((), (), s32[]{:S(2)}) async-start(), calls=%async_computation.12 | async-start | bytes 9437184 | tf_op jit(solution)/shard_map/all_gather | solution.py:129
  271.5 525.5 %all-reduce.8.cloned.1.call-start = ((), (), s32[]{:S(2)}) async-start(), calls=%async_computation.13 | async-start | bytes 16777216 | tf_op jit(solution)/shard_map/psum | solution.py:32
  446.8 594.4 %copy-start.39 = (f32[1024]{0:T(1024)}, f32[1024]{0:T(1024)S(1)}, u32[]{:S(2)}) copy-start(f32[1024]{0:T(1024)S(1)} %broadcast_multiply_fusion.1) | copy-start | bytes 12292
  451.1 590.1 %copy-start.43 = (f32[1024]{0:T(1024)}, f32[1024]{0:T(1024)S(1)}, u32[]{:S(2)}) copy-start(f32[1024]{0:T(1024)S(1)} %fusion.81) | copy-start | bytes 12292
  626.6 402.8 %all-reduce.10.cloned.1.call-start = ((), (), s32[]{:S(2)}) async-start(), calls=%async_computation.14 | async-start | bytes 16777216 | tf_op jit(solution)/shard_map/psum | solution.py:32
  818.5 210.9 %copy-start.53 = (f32[1024]{0:T(1024)}, f32[1024]{0:T(1024)S(1)}, u32[]{:S(2)}) copy-start(f32[1024]{0:T(1024)S(1)} %negate_multiply_fusion.1) | copy-start | bytes 12292
  856.5 529.0 %reduce-scatter.13.cloned.1.call-start = ((), (), s32[]{:S(2)}) async-start(), calls=%async_computation.19 | async-start | bytes 2359296 | tf_op jit(solution)/shard_map/reduce_scatter | solution.py:247
  1060.2 327.1 %reduce-scatter.7.cloned.1.call-start = ((), (), s32[]{:S(2)}) async-start(), calls=%async_computation.16 | async-start | bytes 2359296 | tf_op jit(solution)/shard_map/reduce_scatter | solution.py:238
  1236.0 153.2 %reduce-scatter.11.cloned.1.call-start = ((), (), s32[]{:S(2)}) async-start(), calls=%async_computation.18 | async-start | bytes 2359296 | tf_op jit(solution)/shard_map/reduce_scatter | solution.py:244
  1296.3 4.6 collective-permute-start.7
  1297.6 5.5 collective-permute-start.6
  1307.3 94.0 %reduce-scatter.9.cloned.1.call-start = ((), (), s32[]{:S(2)}) async-start(), calls=%async_computation.17 | async-start | bytes 2359296 | tf_op jit(solution)/shard_map/reduce_scatter | solution.py:241
  1307.3 15.0 collective-permute-start.4
  1319.9 6.7 collective-permute-start.5
  1334.1 157.8 %reduce-scatter.15.cloned.1.call-start = ((), (), s32[]{:S(2)}) async-start(), calls=%async_computation.20 | async-start | bytes 9437184 | tf_op jit(solution)/shard_map/reduce_scatter | solution.py:153
  1349.6 232.5 %reduce-scatter.17.cloned.1.call-start = ((), (), s32[]{:S(2)}) async-start(), calls=%async_computation.21 | async-start | bytes 9437184 | tf_op jit(solution)/shard_map/reduce_scatter | solution.py:156
  1370.3 386.7 %all-reduce.12.cloned.1.call-start = ((), (), s32[]{:S(2)}) async-start(), calls=%async_computation.15 | async-start | bytes 16777216 | tf_op jit(solution)/shard_map/psum | solution.py:32
  1384.1 372.9 %copy-start.46 = (f32[1024]{0:T(1024)S(1)}, f32[1024]{0:T(1024)}, u32[]{:S(2)}) copy-start(f32[1024]{0:T(1024)} %copy-done.45) | copy-start | bytes 12292
  1584.8 182.2 %copy-start.51 = (bf16[2048]{0:T(1024)(128)(2,1)S(1)}, bf16[2048]{0:T(1024)(128)(2,1)}, u32[]{:S(2)}) copy-start(bf16[2048]{0:T(1024)(128)(2,1)} %get-tuple-element.567) | copy-start | bytes 12292
  1584.8 182.2 %copy-start.52 = (bf16[2048]{0:T(1024)(128)(2,1)S(1)}, bf16[2048]{0:T(1024)(128)(2,1)}, u32[]{:S(2)}) copy-start(bf16[2048]{0:T(1024)(128)(2,1)} %get-tuple-element.669) | copy-start | bytes 12292
  1584.9 182.2 %copy-start.64 = (bf16[2048]{0:T(1024)(128)(2,1)S(1)}, bf16[2048]{0:T(1024)(128)(2,1)}, u32[]{:S(2)}) copy-start(bf16[2048]{0:T(1024)(128)(2,1)} %get-tuple-element.672) | copy-start | bytes 12292
  (85 other events, 1895.4 us)
Sparse Core Ops, SparseCore 0:
  10.2 31.7 all-gather.8
  44.2 33.7 all-gather.10
  80.1 37.1 all-gather.6
  119.3 33.6 all-gather.12
  266.0 174.9 all-reduce.5
  443.1 82.7 all-gather.14
  528.1 81.0 all-gather.16
  626.7 170.2 all-reduce.7
  856.6 172.7 all-reduce.9
  1060.3 36.5 reduce-scatter.12
  1236.1 36.5 reduce-scatter.6
  1307.4 52.8 reduce-scatter.10
  1363.2 37.9 reduce-scatter.8
  1403.5 88.3 reduce-scatter.14
  1494.1 87.9 reduce-scatter.16
  1586.5 170.4 all-reduce.11
where the time goes:
time: 1810 us
  waiting for transfers between devices  1100 us (61%)
  matrix products  235 us (13%)
  other arithmetic  222 us (12%)
  local copies, waits for them, and re-layouts  176 us (10%)
  starting transfers between devices  30.5 us (2%)
  blocking collectives  28.6 us (2%)
    psum x4, waiting for transfers between devices, tensor_total(): return lax.psum(part, 'tensor')  684 us
    reduce_scatter x1, waiting for transfers between devices, on_device(): lax.psum_scatter(grad_w_inner.astype(jnp.bfloat16), 'dp', scatter_dimensi...  88.7 us
    reduce_scatter x1, waiting for transfers between devices, on_device(): lax.psum_scatter(grad_w_outer.astype(jnp.bfloat16), 'dp', scatter_dimensi...  87.5 us
    all_gather x1, waiting for transfers between devices, on_device(): lax.all_gather(w_inner.astype(jnp.bfloat16), 'dp', axis=0, tiled=True)  74.8 us
    all_gather x1, waiting for transfers between devices, on_device(): lax.all_gather(w_outer.astype(jnp.bfloat16), 'dp', axis=1, tiled=True)  67.5 us
    select_n x4, other arithmetic, on_device(): key_slab = jnp.where(far_hit, far_key[None], key_slab)  57.8 us
    dot_general x6, matrix products, mat_bf(): return jnp.dot(left, right, preferred_element_type=jnp.float32)  57 us
    reduce_sum x1, other arithmetic, on_device(): send_key = jnp.sum(jnp.where(far_hit, key_grad_slab, 0.0), axis=0)  47.1 us
  transfers between devices with their start and end apart: 24, of which 15 were waited for; matrix products, arithmetic and copies ran while one was open for 26% of the time, Pallas kernels for 0%

commit v1 on v0

--- a/solution.py
+++ b/solution.py
@@ -6,6 +6,22 @@
 HEAD_DIM = 128
 SLOT = 2048
 norm_eps = 1e-12
+
+
+def ring_gather(x, axis, dim):
+    ways, here, step = (lax.axis_size(axis), lax.axis_index(axis), x.shape[dim])
+    shape = [n * ways if d == dim else n for d, n in enumerate(x.shape)]
+    full = lax.dynamic_update_slice_in_dim(jnp.zeros(shape, x.dtype), x, here * step, axis=dim)
+    going_up = going_down = x
+    for far in range(1, ways // 2 + 1):
+        going_up = lax.ppermute(going_up, axis, [(d, (d + 1) % ways) for d in range(ways)])
+        full = lax.dynamic_update_slice_in_dim(full, going_up, (here - far) % ways * step, axis=dim)
+        if 2 * far < ways:
+            going_down = lax.ppermute(going_down, axis, [(d, (d - 1) % ways) for d in range(ways)])
+            full = lax.dynamic_update_slice_in_dim(
+                full, going_down, (here + far) % ways * step, axis=dim
+            )
+    return full
 
 
 def passed_along(value, axis, steps):
@@ -125,7 +141,7 @@
     hidden, norm_one_back = jax.vjp(layer_norm, resid_one, ln1_gain, ln1_bias)
     hidden_low = hidden.astype(jnp.bfloat16)
     full_inner, full_outer = (
-        lax.all_gather(w_inner.astype(jnp.bfloat16), "dp", axis=0, tiled=True),
+        ring_gather(w_inner.astype(jnp.bfloat16), "dp", 0),
         lax.all_gather(w_outer.astype(jnp.bfloat16), "dp", axis=1, tiled=True),
     )
     inner = mat_bf(hidden_low, full_inner) + b_inner

time: 1810 us -> 1770 us (0.978)
  waiting for transfers between devices: 1100 us -> 1010 us
  starting transfers between devices: 30.5 us -> 56.8 us
    psum x4, waiting for transfers between devices: 684 us -> 592 us  [tensor_total(): return lax.psum(part, 'tensor')]
    ppermute x0 -> x7, waiting for transfers between devices: none -> 46.9 us  [the longest x4 45.6 us: ring_gather(): lax.ppermute(going_up, axis, [(d, (d + 1) % ways) for d in range(ways)])]
    all_gather x1, waiting for transfers between devices: 74.8 us -> 38.9 us  [on_device(): lax.all_gather(w_inner.astype(jnp.bfloat16), 'dp', axis=0, tiled=True)]
    ppermute x0 -> x7, starting transfers between devices: none -> 26.4 us  [the longest x4 15.8 us: ring_gather(): lax.ppermute(going_up, axis, [(d, (d + 1) % ways) for d in range(ways)])]
  transfers between devices with their start and end apart: 24 -> 31, of which waited for: 15 -> 20; matrix products, arithmetic and copies ran while one was open for 26% -> 30% of each run, Pallas kernels for 0% -> 0%
where the time goes in v1:
time: 1770 us; the launch traced here: 1760 us
  waiting for transfers between devices  1010 us (57%)
  matrix products  234 us (13%)
  other arithmetic  220 us (12%)
  local copies, waits for them, and re-layouts  192 us (11%)
  starting transfers between devices  56.8 us (3%)
  blocking collectives  28.6 us (2%)
    psum x4, waiting for transfers between devices, tensor_total(): return lax.psum(part, 'tensor')  592 us
    reduce_scatter x1, waiting for transfers between devices, on_device(): lax.psum_scatter(grad_w_inner.astype(jnp.bfloat16), 'dp', scatter_dimensi...  88.6 us
    reduce_scatter x1, waiting for transfers between devices, on_device(): lax.psum_scatter(grad_w_outer.astype(jnp.bfloat16), 'dp', scatter_dimensi...  87.4 us
    all_gather x1, waiting for transfers between devices, on_device(): lax.all_gather(w_outer.astype(jnp.bfloat16), 'dp', axis=1, tiled=True)  62.4 us
    select_n x4, other arithmetic, on_device(): key_slab = jnp.where(far_hit, far_key[None], key_slab)  57.8 us
    dot_general x6, matrix products, mat_bf(): return jnp.dot(left, right, preferred_element_type=jnp.float32)  55.4 us
    reduce_sum x1, other arithmetic, on_device(): send_key = jnp.sum(jnp.where(far_hit, key_grad_slab, 0.0), axis=0)  47 us
    ppermute x4, waiting for transfers between devices, ring_gather(): lax.ppermute(going_up, axis, [(d, (d + 1) % ways) for d in range(ways)])  45.6 us
  transfers between devices with their start and end apart: 31, of which 20 were waited for; matrix products, arithmetic and copies ran while one was open for 30% of the time, Pallas kernels for 0%

profile of v1, /device:TPU:0, one launch (start us, length us, event | category | flops | bytes accessed | tf_op | source)
XLA Modules:
  0.0 1762.6 jit_solution(12653273118603010585)
XLA Ops:
  14.7 27.4 %all-gather.9.cloned.1.call-done = bf16[2048,512]{1,0:T(8,128)(2,1)} async-done(((bf16[256,512]{1,0:T(8,128)(2,1)}), bf16[2048,512]{1,0:T(8,128)(2,1)}) %all-gather.9.cloned.1.call-update) | async-done | bytes 2097168 | tf_op jit(solution)/shard_map/all_gather | solution.py:96
  52.7 25.2 %all-gather.11.cloned.1.call-done = bf16[2048,512]{1,0:T(8,128)(2,1)} async-done(((bf16[256,512]{1,0:T(8,128)(2,1)}), bf16[2048,512]{1,0:T(8,128)(2,1)}) %all-gather.11.cloned.1.call-update) | async-done | bytes 2097168 | tf_op jit(solution)/shard_map/all_gather | solution.py:97
  90.8 26.6 %all-gather.7.cloned.1.call-done = bf16[2048,512]{1,0:T(8,128)(2,1)} async-done(((bf16[256,512]{1,0:T(8,128)(2,1)}), bf16[2048,512]{1,0:T(8,128)(2,1)}) %all-gather.7.cloned.1.call-update) | async-done | bytes 2097168 | tf_op jit(solution)/shard_map/all_gather | solution.py:95
  127.7 128.2 %while.31 = (s32[]{:T(128)}, bf16[2,512,4,128]{3,1,2,0:T(8,128)(2,1)}, f32[2,4,512,1]{2,1,3,0:T(4,128)S(1)}, bf16[2,512,4,128]{3,1,2,0:T(8,128)(2,1)}, s32[]{:T(...) while((s32[]{:T(128)}, ...), condition=%wide.region_5.6_spmd.clone.clone, body=%wide.region_2.5_spmd.clone.clone.sunk | while | flops 2204106752 | bytes 137967920 | solution.py:136
  164.8 14.5 select_select_fusion.6
  228.9 14.5 select_select_fusion.6
  278.6 20.0 %collective-permute-done.4 = bf16[256,2048]{1,0:T(8,128)(2,1)S(1)} collective-permute-done((bf16[256,2048]{1,0:T(8,128)(2,1)S(1)}, bf16[256,2048]{1,0:T(8,128)(2,1)S(1)}, u32[]{:S(2)}, u32[]{:S(2)}) %collective-permute-start.4) | collective-permute-done | bytes 1048608 | tf_op jit(solution)/shard_map/ppermute | solution.py:17
  305.5 15.1 collective-permute-done.6
  360.8 80.8 %all-reduce.6.cloned.1.call-done = f32[1024,2048]{1,0:T(8,128)} async-done(((f32[1024,2048]{1,0:T(8,128)}), f32[1024,2048]{1,0:T(8,128)}) %all-reduce.6.cloned.1.call-update) | async-done | bytes 8388624 | tf_op jit(solution)/shard_map/psum | solution.py:48
  450.5 13.9 fusion.87
  464.4 62.4 %all-gather.15.cloned.1.call-done = bf16[2048,2048]{1,0:T(8,128)(2,1)} async-done(((bf16[2048,256]{1,0:T(8,128)(2,1)}), bf16[2048,2048]{1,0:T(8,128)(2,1)}) %all-gather.15.cloned.1.call-update) | async-done | bytes 8388624 | tf_op jit(solution)/shard_map/all_gather | solution.py:145
  526.8 17.3 fusion.85
  545.8 168.9 %all-reduce.8.cloned.1.call-done = f32[1024,2048]{1,0:T(8,128)} async-done(((f32[1024,2048]{1,0:T(8,128)}), f32[1024,2048]{1,0:T(8,128)}) %all-reduce.8.cloned.1.call-update) | async-done | bytes 8388624 | tf_op jit(solution)/shard_map/psum | solution.py:48
  736.4 23.8 %fusion.94 = (bf16[2048]{0:T(1024)(128)(2,1)}, bf16[1024,2048]{1,0:T(8,128)(2,1)}) fusion(bf16[2048,2048]{1,0:T(8,128)(2,1)} %all-gather.15.cloned.1.call-done, f32[1024,2048]{1,0:T(8,128)} %get-tuple-element.655, f32[1024]{0:T(1024)S(1)} %negate_multiply_fusion.1, f32[1024,2048]{1,0:T(8,128)} %fusion.87, f32[2048]{0:T(1024)S(1)} %copy-done.73), kind=kOutput, calls=%fused_computation.157 | convolution fusion | flops 8648652800 | bytes 29376512 | tf_op jit(solution)/shard_map/td,fd->tf/dot_general | solution.py:161
  760.1 38.9 %all-gather.17.cloned.1.call-done = bf16[2048,2048]{1,0:T(8,128)(2,1)} async-done(((bf16[256,2048]{1,0:T(8,128)(2,1)}), bf16[2048,2048]{1,0:T(8,128)(2,1)}) %all-gather.17.cloned.1.call-update) | async-done | bytes 8388624 | tf_op jit(solution)/shard_map/all_gather | solution.py:155
  799.0 14.6 fusion.95
  813.7 170.7 %all-reduce.10.cloned.1.call-done = f32[1024,2048]{1,0:T(8,128)} async-done(((f32[1024,2048]{1,0:T(8,128)}), f32[1024,2048]{1,0:T(8,128)}) %all-reduce.10.cloned.1.call-update) | async-done | bytes 8388624 | tf_op jit(solution)/shard_map/psum | solution.py:48
  1016.4 165.6 %while.32 = (s32[]{:T(128)}, f32[2048,4,128]{0,2,1:T(8,128)}, f32[2048,4,128]{0,2,1:T(8,128)}, bf16[2,512,4,128]{3,1,2,0:T(8,128)(2,1)}, bf16[2,512,4,128]{3,1,2...) while((s32[]{:T(128)}, f32[2048,4,128]{0,2,1:T(8,128)}, ...), condition=%wide.region_19.20_spmd.clone.clone.clone, body=%wide.region_17.19_spmd.clone.clone.clone.sunk | while | flops 5443420160 | bytes 367073888 | solution.py:220
  1037.2 14.4 select_select_fusion.7
  1066.7 11.6 multiply_reduce_fusion.8
  1078.3 12.9 multiply_convert_fusion.5
  1118.9 14.4 select_select_fusion.7
  1150.0 11.6 multiply_reduce_fusion.8
  1161.6 12.9 multiply_convert_fusion.5
  1204.1 47.0 %select_reduce_fusion.4 = (bf16[1024,512]{0,1:T(8,128)(2,1)}, bf16[1024,512]{0,1:T(8,128)(2,1)}, f32[1024,512]{0,1:T(8,128)S(1)}, f32[1024,512]{0,1:T(8,128)S(1)...) fusion(f32[2,1024,512]{1,0,2:T(2,128)} %reshape.188, pred[2]{0:T(512)(128)(4,1)S(1)} %copy-done.68, ...), kind=kLoop, calls=%fused_computation.97 | loop fusion | flops 9437184 | bytes 16777222 | tf_op jit(solution)/shard_map/reduce_sum | solution.py:229
  1262.4 12.6 collective-permute-start.11
  1289.2 15.4 convolution_convert_fusion.1
  1305.4 20.0 %convolution_convert_fusion = bf16[2048,2048]{1,0:T(8,128)(2,1)} fusion(f32[1024,2048]{1,0:T(8,128)} %get-tuple-element.655, f32[1024]{0:T(1024)S(1)} %copy-done.59, f32[1024,2048]{1,0:T(8,128)} %fusion.87, f32[2048]{0:T(1024)S(1)} %copy-done.74), kind=kOutput, calls=%fused_computation.84 | convolution fusion | flops 8619294720 | bytes 25178112 | tf_op jit(solution)/shard_map/tf,td->fd/dot_general | solution.py:160
  1358.2 88.6 %reduce-scatter.15.cloned.1.call-done = bf16[256,2048]{1,0:T(8,128)(2,1)} async-done(((bf16[2048,2048]{1,0:T(8,128)(2,1)}), bf16[256,2048]{1,0:T(8,128)(2,1)}) %reduce-scatter.15.cloned.1.call-update) | async-done | bytes 1048592 | tf_op jit(solution)/shard_map/reduce_scatter | solution.py:169
  1449.6 87.4 %reduce-scatter.17.cloned.1.call-done = bf16[2048,256]{1,0:T(8,128)(2,1)} async-done(((bf16[2048,2048]{1,0:T(8,128)(2,1)}), bf16[2048,256]{1,0:T(8,128)(2,1)}) %reduce-scatter.17.cloned.1.call-update) | async-done | bytes 1048592 | tf_op jit(solution)/shard_map/reduce_scatter | solution.py:172
  1539.8 172.2 %all-reduce.12.cloned.1.call-done = f32[1024,2048]{1,0:T(8,128)} async-done(((f32[1024,2048]{1,0:T(8,128)}), f32[1024,2048]{1,0:T(8,128)}) %all-reduce.12.cloned.1.call-update) | async-done | bytes 8388624 | tf_op jit(solution)/shard_map/psum | solution.py:48
  1722.0 28.6 %all-reduce = (bf16[512]{0:T(512)(128)(2,1)S(1)}, bf16[512]{0:T(512)(128)(2,1)S(1)}, bf16[2048]{0:T(1024)(128)(2,1)S(1)}, bf16[2048]{0:T(1024)(128)(2,1)S(1)}, b...) all-reduce(bf16[512]{0:T(512)(128)(2,1)S(1)} %bitcast.117, ...), channel_id=1, replica_groups=mesh['dp'=8,'tensor'=4] {'dp'}, use_global_device_ids=true, to_apply=%region_31.32 | all-reduce | flops 15360 | bytes 61440 | tf_op jit(solution)/shard_map/psum | solution.py:278
  (416 shorter events, 462.3 us)
Async XLA Ops:
  7.2 34.8 %all-gather.9.cloned.1.call-start = ((), (), s32[]{:S(2)}) async-start(), calls=%async_computation.7 | async-start | bytes 2359296 | tf_op jit(solution)/shard_map/all_gather | solution.py:96
  9.0 68.9 %all-gather.11.cloned.1.call-start = ((), (), s32[]{:S(2)}) async-start(), calls=%async_computation.8 | async-start | bytes 2359296 | tf_op jit(solution)/shard_map/all_gather | solution.py:97
  10.9 106.5 %all-gather.7.cloned.1.call-start = ((), (), s32[]{:S(2)}) async-start(), calls=%async_computation.6 | async-start | bytes 2359296 | tf_op jit(solution)/shard_map/all_gather | solution.py:95
  12.7 246.0 %all-gather.13.cloned.1.call-start = ((), (), s32[]{:S(2)}) async-start(), calls=%async_computation.9 | async-start | bytes 2359296 | tf_op jit(solution)/shard_map/all_gather | solution.py:98
  14.6 426.9 %all-reduce.6.cloned.1.call-start = ((), (), s32[]{:S(2)}) async-start(), calls=%async_computation.10 | async-start | bytes 16777216 | tf_op jit(solution)/shard_map/psum | solution.py:48
  47.3 79.3 %collective-permute-start.1 = (bf16[1024,512]{1,0:T(8,128)(2,1)S(1)}, bf16[1024,512]{1,0:T(8,128)(2,1)}, u32[]{:S(2)}, u32[]{:S(2)}) collective-permute-start(bf16[1024,512]{1,0:T(8,128)(2,1)S(1)} %convolution_convert_fusion.7), channel_id=1, source_target_pairs={{4,0},{8,4},{12,8},{16,12},{20,16},{24,20},{28,24},{5,1},{9,5},{13... | collective-permute-start | bytes 3145736 | tf_op jit(solution)/shard_map/ppermute | solution.py:30
  48.7 77.8 %collective-permute-start = (bf16[1024,512]{1,0:T(8,128)(2,1)S(1)}, bf16[1024,512]{1,0:T(8,128)(2,1)}, u32[]{:S(2)}, u32[]{:S(2)}) collective-permute-start(bf16[1024,512]{1,0:T(8,128)(2,1)S(1)} %convolution_convert_fusion.7), channel_id=1, source_target_pairs={{0,4},{4,8},{8,12},{12,16},{16,20},{20,24},{24,28},{1,5},{5,9},{9,... | collective-permute-start | bytes 3145736 | tf_op jit(solution)/shard_map/ppermute | solution.py:30
  83.2 43.4 %collective-permute-start.3 = (bf16[1024,512]{1,0:T(8,128)(2,1)S(1)}, bf16[1024,512]{1,0:T(8,128)(2,1)}, u32[]{:S(2)}, u32[]{:S(2)}) collective-permute-start(bf16[1024,512]{1,0:T(8,128)(2,1)S(1)} %add_convert_fusion.4), channel_id=1, source_target_pairs={{4,0},{8,4},{12,8},{16,12},{20,16},{24,20},{28,24},{5,1},{9,5},{13... | collective-permute-start | bytes 3145736 | tf_op jit(solution)/shard_map/ppermute | solution.py:30
  84.5 42.1 %collective-permute-start.2 = (bf16[1024,512]{1,0:T(8,128)(2,1)S(1)}, bf16[1024,512]{1,0:T(8,128)(2,1)}, u32[]{:S(2)}, u32[]{:S(2)}) collective-permute-start(bf16[1024,512]{1,0:T(8,128)(2,1)S(1)} %add_convert_fusion.4), channel_id=1, source_target_pairs={{0,4},{4,8},{8,12},{12,16},{16,20},{20,24},{24,28},{1,5},{5,9},{9,... | collective-permute-start | bytes 3145736 | tf_op jit(solution)/shard_map/ppermute | solution.py:30
  266.5 260.3 %all-gather.15.cloned.1.call-start = ((), (), s32[]{:S(2)}) async-start(), calls=%async_computation.11 | async-start | bytes 9437184 | tf_op jit(solution)/shard_map/all_gather | solution.py:145
  269.3 445.3 %all-reduce.8.cloned.1.call-start = ((), (), s32[]{:S(2)}) async-start(), calls=%async_computation.12 | async-start | bytes 16777216 | tf_op jit(solution)/shard_map/psum | solution.py:48
  275.0 23.5 %collective-permute-start.4 = (bf16[256,2048]{1,0:T(8,128)(2,1)S(1)}, bf16[256,2048]{1,0:T(8,128)(2,1)S(1)}, u32[]{:S(2)}, u32[]{:S(2)}) collective-permute-start(bf16[256,2048]{1,0:T(8,128)(2,1)S(1)} %get-tuple-element.661), channel_id=1, source_target_pairs={{0,4},{4,8},{8,12},{12,16},{16,20},{20,24},{24,28},{28,0},{1,5},{5... | collective-permute-start | bytes 3145736 | tf_op jit(solution)/shard_map/ppermute | solution.py:17
  275.2 27.0 %collective-permute-start.5 = (bf16[256,2048]{1,0:T(8,128)(2,1)S(1)}, bf16[256,2048]{1,0:T(8,128)(2,1)S(1)}, u32[]{:S(2)}, u32[]{:S(2)}) collective-permute-start(bf16[256,2048]{1,0:T(8,128)(2,1)S(1)} %get-tuple-element.661), channel_id=1, source_target_pairs={{0,28},{4,0},{8,4},{12,8},{16,12},{20,16},{24,20},{28,24},{1,29},{... | collective-permute-start | bytes 3145736 | tf_op jit(solution)/shard_map/ppermute | solution.py:20
  298.5 22.1 %collective-permute-start.6 = (bf16[256,2048]{1,0:T(8,128)(2,1)S(1)}, bf16[256,2048]{1,0:T(8,128)(2,1)}, u32[]{:S(2)}, u32[]{:S(2)}) collective-permute-start(bf16[256,2048]{1,0:T(8,128)(2,1)S(1)} %collective-permute-done.4), channel_id=1, source_target_pairs={{0,4},{4,8},{8,12},{12,16},{16,20},{20,24},{24,28},{28,0},{1,5},{5... | collective-permute-start | bytes 3145736 | tf_op jit(solution)/shard_map/ppermute | solution.py:17
  302.3 25.4 %collective-permute-start.7 = (bf16[256,2048]{1,0:T(8,128)(2,1)S(1)}, bf16[256,2048]{1,0:T(8,128)(2,1)}, u32[]{:S(2)}, u32[]{:S(2)}) collective-permute-start(bf16[256,2048]{1,0:T(8,128)(2,1)S(1)} %collective-permute-done.5), channel_id=1, source_target_pairs={{0,28},{4,0},{8,4},{12,8},{16,12},{20,16},{24,20},{28,24},{1,29},{... | collective-permute-start | bytes 3145736 | tf_op jit(solution)/shard_map/ppermute | solution.py:20
  320.7 21.8 %collective-permute-start.8 = (bf16[256,2048]{1,0:T(8,128)(2,1)}, bf16[256,2048]{1,0:T(8,128)(2,1)}, u32[]{:S(2)}, u32[]{:S(2)}) collective-permute-start(bf16[256,2048]{1,0:T(8,128)(2,1)} %collective-permute-done.6), channel_id=1, source_target_pairs={{0,4},{4,8},{8,12},{12,16},{16,20},{20,24},{24,28},{28,0},{1,5},{5... | collective-permute-start | bytes 3145736 | tf_op jit(solution)/shard_map/ppermute | solution.py:17
  327.6 29.2 %collective-permute-start.9 = (bf16[256,2048]{1,0:T(8,128)(2,1)}, bf16[256,2048]{1,0:T(8,128)(2,1)S(1)}, u32[]{:S(2)}, u32[]{:S(2)}) collective-permute-start(bf16[256,2048]{1,0:T(8,128)(2,1)} %collective-permute-done.7), channel_id=1, source_target_pairs={{0,28},{4,0},{8,4},{12,8},{16,12},{20,16},{24,20},{28,24},{1,29},{... | collective-permute-start | bytes 3145736 | tf_op jit(solution)/shard_map/ppermute | solution.py:20
  342.5 17.2 collective-permute-start.10
  447.3 548.7 %copy-start.44 = (f32[1024]{0:T(1024)}, f32[1024]{0:T(1024)S(1)}, u32[]{:S(2)}) copy-start(f32[1024]{0:T(1024)S(1)} %broadcast_multiply_fusion.1) | copy-start | bytes 12292
  544.2 254.8 %all-gather.17.cloned.1.call-start = ((), (), s32[]{:S(2)}) async-start(), calls=%async_computation.13 | async-start | bytes 9437184 | tf_op jit(solution)/shard_map/all_gather | solution.py:155
  544.9 439.5 %all-reduce.10.cloned.1.call-start = ((), (), s32[]{:S(2)}) async-start(), calls=%async_computation.14 | async-start | bytes 16777216 | tf_op jit(solution)/shard_map/psum | solution.py:48
  813.7 527.0 %reduce-scatter.13.cloned.1.call-start = ((), (), s32[]{:S(2)}) async-start(), calls=%async_computation.19 | async-start | bytes 2359296 | tf_op jit(solution)/shard_map/reduce_scatter | solution.py:263
  1015.2 327.3 %reduce-scatter.7.cloned.1.call-start = ((), (), s32[]{:S(2)}) async-start(), calls=%async_computation.16 | async-start | bytes 2359296 | tf_op jit(solution)/shard_map/reduce_scatter | solution.py:254
  1190.9 153.5 %reduce-scatter.11.cloned.1.call-start = ((), (), s32[]{:S(2)}) async-start(), calls=%async_computation.18 | async-start | bytes 2359296 | tf_op jit(solution)/shard_map/reduce_scatter | solution.py:260
  1251.2 4.8 collective-permute-start.14
  1252.4 5.7 collective-permute-start.13
  1262.4 94.0 %reduce-scatter.9.cloned.1.call-start = ((), (), s32[]{:S(2)}) async-start(), calls=%async_computation.17 | async-start | bytes 2359296 | tf_op jit(solution)/shard_map/reduce_scatter | solution.py:257
  1262.4 15.0 collective-permute-start.11
  1275.0 6.7 collective-permute-start.12
  1289.2 157.7 %reduce-scatter.15.cloned.1.call-start = ((), (), s32[]{:S(2)}) async-start(), calls=%async_computation.20 | async-start | bytes 9437184 | tf_op jit(solution)/shard_map/reduce_scatter | solution.py:169
  1304.7 232.3 %reduce-scatter.17.cloned.1.call-start = ((), (), s32[]{:S(2)}) async-start(), calls=%async_computation.21 | async-start | bytes 9437184 | tf_op jit(solution)/shard_map/reduce_scatter | solution.py:172
  1325.5 386.5 %all-reduce.12.cloned.1.call-start = ((), (), s32[]{:S(2)}) async-start(), calls=%async_computation.15 | async-start | bytes 16777216 | tf_op jit(solution)/shard_map/psum | solution.py:48
  (97 other events, 3666.8 us)
Sparse Core Ops, SparseCore 0:
  10.2 31.7 all-gather.8
  44.2 33.7 all-gather.10
  80.1 37.2 all-gather.6
  119.4 33.6 all-gather.12
  266.6 174.8 all-reduce.5
  443.6 83.1 all-gather.14
  544.3 170.2 all-reduce.7
  716.2 82.7 all-gather.16
  813.8 170.6 all-reduce.9
  1015.3 36.5 reduce-scatter.12
  1191.0 36.5 reduce-scatter.6
  1262.5 52.8 reduce-scatter.10
  1318.3 37.9 reduce-scatter.8
  1358.6 88.2 reduce-scatter.14
  1449.1 87.9 reduce-scatter.16
  1541.4 170.4 all-reduce.11
